TPU v7x, 32 devices: a whole 2x2x4 slice. The times are simulated.
32 devices in a mesh: seq: 16 (over z, y, x), head: 2 (over core).
Axes of the slice: x: 2, y: 2, z: 4, core: 2. Of those that a mesh axis runs over, the one named last changes fastest.
Arguments:
- x_inner: bfloat16 [2, 8192, 5120], P(None, 'seq', 'head'), may hold values from -6 to 6
- z_gate: bfloat16 [2, 8192, 5120], P(None, 'seq', 'head'), may hold values from -200 to 200
- b_input: bfloat16 [2, 8192, 128], P(None, 'seq'), may hold values from -6 to 6
- c_output: bfloat16 [2, 8192, 128], P(None, 'seq'), may hold values from -6 to 6
- step_sizes: float32 [2, 8192, 80], P(None, 'seq', 'head'), may hold values from 0.0002 to 0.2
- decay_log: float32 [80], P('head'), may hold values from -20 to 2
- skip_gain: float32 [80], P('head'), may hold values from 1 to 4
- norm_gain: float32 [5120], P('head'), may hold values from 0.5 to 1.5
- goal_pos: int32 [2, 512], P(None, 'seq'), may hold values from 0 to 8191, as said below
- goal_owner: int32 [2, 512], P(None, 'seq'), may hold values from 0 to 15, as said below
- value_w1: bfloat16 [16, 5120, 1024], P('seq', None, 'head'), may hold values from -0.078125 to 0.078125
- value_b1: float32 [16, 1024], P('seq', 'head'), may hold values from -3 to 3
- value_w2: bfloat16 [16, 1024], P('seq', 'head'), may hold values from -0.1875 to 0.1875
Outputs:
- layer_out: bfloat16 [2, 8192, 5120], P(None, 'seq', 'head')
- values: float32 [2, 512], P(None, 'seq')
Inputs may be any that keep to these rules, and one draw needn't show every extreme that they name: For every sequence s and every b, goal_pos[s, b * 32 + i] for i < 32 are distinct positions from b * 512 to (b + 1) * 512 - 1, increasing in i. `goal_owner`: among the 2 x 32 goals of the columns b * 32 to (b + 1) * 32 - 1, no expert is named more than 4 times; one expert is named exactly 4 times in every such group of columns.
All inputs are finite; a program needn't handle non-finite values.
Results may differ from a plain program's by a relative error of at most 0.0056.
Values may be sent and summed in bfloat16 or wider, within the bound.
No kernel may reach another device: no remote copies, remote signals or barrier semaphores. Data moves between devices by JAX's collectives and lax.ppermute only.
A program may use at most 384 MiB of HBM per device.

v0:
```python
import jax
import jax.numpy as jnp
from jax import lax
from jax.sharding import PartitionSpec as P

HEAD_TOTAL = 80
HEAD_DIM = 64
BLOCK = 256
CAP = 4
norm_eps = 1e-05


def carried_in(value, axis, combine, identity):
    length, index = (lax.axis_size(axis), lax.axis_index(axis))
    everything = jax.tree.map(lambda part: lax.all_gather(part, axis), value)
    start = jax.tree.map(
        lambda part, zero: jnp.broadcast_to(jnp.asarray(zero, part.dtype), part.shape),
        value,
        identity,
    )

    def hop(k, before):
        reached = k < index
        new = combine(before, jax.tree.map(lambda part: part[k], everything))
        return jax.tree.map(lambda a, b: jnp.where(reached, a, b), new, before)

    return lax.fori_loop(0, length, hop, start)


def block_parts(x_seq, b_seq, c_seq, dt_seq, decay_rates):
    length = x_seq.shape[0]
    head_count = dt_seq.shape[1]
    block_count = length // BLOCK
    x_blocks = x_seq.reshape(block_count, BLOCK, head_count, -1)
    b_blocks = b_seq.reshape(block_count, BLOCK, -1)
    c_blocks = c_seq.reshape(block_count, BLOCK, -1)
    dt_blocks = jnp.transpose(dt_seq.reshape(block_count, BLOCK, head_count), (0, 2, 1))
    cumulative = jnp.cumsum(dt_blocks * decay_rates[None, :, None], axis=2)
    end_weights = jnp.exp(cumulative[:, :, -1:] - cumulative) * dt_blocks
    x_weighted = (x_blocks * jnp.transpose(end_weights, (0, 2, 1))[..., None]).astype(jnp.bfloat16)
    states = jnp.einsum("crhp,crn->chpn", x_weighted, b_blocks, preferred_element_type=jnp.float32)
    return (x_blocks, b_blocks, c_blocks, dt_blocks, cumulative, states)


def diagonal_part(x_blocks, b_blocks, c_blocks, dt_blocks, cumulative):
    routing_scores = jnp.einsum(
        "ckn,crn->ckr", c_blocks, b_blocks, preferred_element_type=jnp.float32
    )
    positions = jnp.arange(BLOCK)
    lower_mask = positions[:, None] >= positions[None, :]
    spread = cumulative[:, :, :, None] - cumulative[:, :, None, :]
    decay_mat = jnp.exp(jnp.where(lower_mask, spread, -jnp.inf))
    weights = (routing_scores[:, None] * decay_mat * dt_blocks[:, :, None, :]).astype(jnp.bfloat16)
    return jnp.einsum("chkr,crhp->ckhp", weights, x_blocks, preferred_element_type=jnp.float32)


def chain_combine(earlier, later):
    return (earlier[0] + later[0], jnp.exp(later[0])[..., None, None] * earlier[1] + later[1])


def pick_rows(layer_seq, index_seq):
    return jnp.take(layer_seq, index_seq, axis=0)


def value_terms(full_rows, value_w1, value_b1, value_w2):
    hidden = (
        jnp.einsum("sjw,wv->sjv", full_rows, value_w1[0], preferred_element_type=jnp.float32)
        + value_b1[0]
    )
    hidden = jax.nn.gelu(hidden).astype(jnp.bfloat16)
    return jnp.einsum("sjv,v->sj", hidden, value_w2[0], preferred_element_type=jnp.float32)


def finish_values(partial_sum):
    partial_sum = lax.psum(partial_sum, "head")
    return lax.all_to_all(partial_sum, "seq", split_axis=0, concat_axis=0, tiled=True)


def body(
    x_inner,
    z_gate,
    b_input,
    c_output,
    step_sizes,
    decay_log,
    skip_gain,
    norm_gain,
    goal_pos,
    goal_owner,
    value_w1,
    value_b1,
    value_w2,
):
    decay_rates = -jnp.exp(decay_log)
    seq_count = x_inner.shape[0]
    length = x_inner.shape[1]
    stored = []
    decay_sums = []
    state_sums = []
    for seq_index in range(seq_count):
        pieces = block_parts(
            x_inner[seq_index],
            b_input[seq_index],
            c_output[seq_index],
            step_sizes[seq_index],
            decay_rates,
        )
        totals = pieces[4][:, :, -1]
        entering = [jnp.zeros_like(pieces[5][0])]
        for block_index in range(totals.shape[0]):
            entering.append(
                jnp.exp(totals[block_index])[:, None, None] * entering[-1] + pieces[5][block_index]
            )
        stored.append((pieces, totals, entering))
        decay_sums.append(jnp.sum(totals, axis=0))
        state_sums.append(entering[-1])
    summary = (jnp.stack(decay_sums), jnp.stack(state_sums))
    identity = (jnp.zeros_like(summary[0]), jnp.zeros_like(summary[1]))
    incoming = carried_in(summary, "seq", chain_combine, identity)[1]
    outputs = []
    for seq_index in range(seq_count):
        pieces, totals, entering = stored[seq_index]
        x_blocks, b_blocks, c_blocks, dt_blocks, cumulative, states = pieces
        y_diag = diagonal_part(x_blocks, b_blocks, c_blocks, dt_blocks, cumulative)
        prior = jnp.cumsum(totals, axis=0) - totals
        carried = (
            jnp.exp(prior)[:, :, None, None] * incoming[seq_index][None] + jnp.stack(entering[:-1])
        ).astype(jnp.bfloat16)
        y_off = (
            jnp.einsum("ckn,chpn->ckhp", c_blocks, carried, preferred_element_type=jnp.float32)
            * jnp.exp(jnp.transpose(cumulative, (0, 2, 1)))[..., None]
        )
        y_all = y_diag + y_off + skip_gain[None, None, :, None] * x_blocks
        outputs.append(y_all.reshape(length, -1))
    y_full = jnp.stack(outputs)
    gated_out = y_full * jax.nn.silu(z_gate.astype(jnp.float32))
    squares = lax.psum(jnp.sum(gated_out * gated_out, axis=-1), "head")
    inv_rms = lax.rsqrt(squares / (HEAD_TOTAL * HEAD_DIM) + norm_eps)
    layer_out = (gated_out * inv_rms[..., None] * norm_gain).astype(jnp.bfloat16)
    goal_dev = goal_pos.shape[1]
    local_pos = goal_pos - lax.axis_index("seq") * length
    picked_rows = jax.vmap(pick_rows)(layer_out, local_pos).reshape(seq_count * goal_dev, -1)
    owners = goal_owner.reshape(-1)
    row_ids = jnp.arange(owners.shape[0])
    same_owner = (owners[:, None] == owners[None, :]) & (row_ids[None, :] < row_ids[:, None])
    slot_rank = jnp.sum(same_owner.astype(jnp.int32), axis=1)
    slot_index = owners * CAP + slot_rank
    experts = lax.axis_size("seq")
    slot_numbers = jnp.arange(experts * CAP)
    placing = (slot_numbers[:, None] == slot_index[None, :]).astype(jnp.bfloat16)
    whole_rows = lax.all_gather(picked_rows, "head", axis=1, tiled=True)
    routed_full = (
        jnp.dot(placing, whole_rows, preferred_element_type=jnp.float32)
        .astype(jnp.bfloat16)
        .reshape(experts, CAP, -1)
    )
    returned = finish_values(
        value_terms(
            lax.all_to_all(routed_full, "seq", split_axis=0, concat_axis=0, tiled=True),
            value_w1,
            value_b1,
            value_w2,
        )
    )
    picked = jnp.take(returned.reshape(-1), slot_index)
    values = picked.reshape(seq_count, goal_dev)
    return (layer_out, values)


def solution(mesh):
    placed = (
        P(None, "seq", "head"),
        P(None, "seq", "head"),
        P(None, "seq", None),
        P(None, "seq", None),
        P(None, "seq", "head"),
        P("head"),
        P("head"),
        P("head"),
        P(None, "seq"),
        P(None, "seq"),
        P("seq", None, "head"),
        P("seq", "head"),
        P("seq", "head"),
    )
    return jax.shard_map(
        body,
        mesh=mesh,
        in_specs=placed,
        out_specs=(P(None, "seq", "head"), P(None, "seq")),
        check_vma=False,
    )
```

profile of v0, /device:TPU:0, one launch (start us, length us, event | category | flops | bytes accessed | tf_op | source)
XLA Modules:
  0.0 669.2 jit_solution(8477946099829321307)
XLA Ops:
  7.2 0.9 fusion.97
  9.2 1.2 reduce-window.14
  10.7 0.8 slice_reduce_fusion.5
  11.5 0.8 fusion.81
  12.4 1.2 reduce-window.16
  13.9 0.8 slice_reduce_fusion.3
  14.6 0.8 fusion.78
  15.7 4.4 fusion.94
  20.0 7.5 %reshape.263 = bf16[2,256,40,64]{3,2,1,0:T(8,128)(2,1)} reshape(bf16[1,512,2560]{2,1,0:T(8,128)(2,1)} %get-tuple-element.139) | data formatting | bytes 5242880 | tf_op jit(solution)/shard_map/reshape;squeeze | solution.py:34
  27.6 6.4 copy.99
  34.0 1.0 fusion.96
  35.2 4.4 reshape.264
  39.6 5.2 copy.107
  44.8 3.5 fusion.29
  48.4 0.9 fusion.27
  49.3 1.9 slice_add_fusion
  51.2 1.8 pad_maximum_fusion
  56.4 0.8 eq.12
  57.8 44.9 %all-gather.2 = f32[16,2,40]{2,1,0:T(2,128)} all-gather(f32[1,2,40]{2,1,0:T(2,128)S(1)} %maximum_bitcast_fusion), channel_id=2, replica_groups=mesh['seq'=16,'head'=2] {'seq'}, dimensions={0}, use_global_device_ids=true | all-gather | bytes 5440 | tf_op jit(solution)/shard_map/all_gather | solution.py:15
  104.1 1.3 subtract_exponential_fusion.1
  107.6 1.0 fusion.95
  108.5 1.0 fusion.98
  109.6 1.0 fusion.99
  110.6 375.5 %all-gather.5.cloned.1.call-done = f32[32,40,64,128]{3,2,1,0:T(8,128)} async-done(((f32[2,40,64,128]{3,2,1,0:T(8,128)}), f32[32,40,64,128]{3,2,1,0:T(8,128)}) %all-gather.5.cloned.1.call-update) | async-done | bytes 41943056 | tf_op jit(solution)/shard_map/all_gather | solution.py:15
  486.1 48.5 %while.14 = (s32[]{:T(128)}, f32[2,40,64,128]{3,2,1,0:T(8,128)S(1)}, s32[]{:T(128)}, f32[16,2,40]{2,1,0:T(2,128)}, f32[16,2,40,64,128]{4,3,2,1,0:T(8,128)}, /*index=5*/s32[]{:T(128)}, s32[]{:T(128)}) while((s32[]{:T(128)}, f32[2,40,64,128]{3,2,1,0:T(8,128)S(1)}, s32[]{:T(128)}, f32[16,2,40]{2,1,0:T(2,128)}, ...), condition=%wide.region_8.9_spmd.clone, body=%wide.region_7.8_spmd.clone.sunk | while | flops 2621444 | bytes 7865385 | solution.py:27
  486.7 2.4 fusion.112
  489.8 2.4 fusion.112
  492.8 2.4 fusion.112
  495.8 2.4 fusion.112
  498.9 2.4 fusion.112
  501.9 2.4 fusion.112
  505.0 2.4 fusion.112
  508.0 2.4 fusion.112
  511.0 2.4 fusion.112
  514.0 2.4 fusion.112
  517.1 2.4 fusion.112
  520.1 2.4 fusion.112
  523.1 2.4 fusion.112
  526.1 2.4 fusion.112
  529.2 2.4 fusion.112
  532.2 2.4 fusion.112
  534.6 1.3 slice_bitcast_fusion.1
  536.2 0.9 fusion.33
  537.8 7.9 %fusion.20 = f32[2,256,40,64]{1,3,2,0:T(8,128)} fusion(bf16[2,256,40,64]{1,3,2,0:T(8,128)(2,1)S(1)} %copy-done.4, f32[2,40,64,256]{3,2,1,0:T(8,128)S(1)} %fusion.33, f32[40]{0:T(128)S(1)} %copy-done.25, f32[2,256,40]{1,2,0:T(8,128)S(1)} %copy-done.10, f32[2,40,256]{2,1,0:T(8,128)S(1)} %copy.97, f32[2,40,256]{2,1,0:T(8,128)S(1)} %copy_bitcast_fusion.1, ...), kind=kOutput, calls=%fused_computation.35 | convolution fusion | flops 703856640 | bytes 13942944 | tf_op jit(solution)/shard_map/chkr,crhp->ckhp/dot_general | solution.py:54
  545.7 8.6 %copy.124 = f32[2,256,40,64]{3,2,1,0:T(8,128)} copy(f32[2,256,40,64]{1,3,2,0:T(8,128)} %fusion.20) | data formatting | bytes 10485760 | tf_op jit(solution)/shard_map/stack;reshape | solution.py:135
  554.4 9.7 %reshape.260 = f32[1,512,2560]{2,1,0:T(8,128)} reshape(f32[2,256,40,64]{3,2,1,0:T(8,128)} %copy.124) | data formatting | bytes 10485760 | tf_op jit(solution)/shard_map/stack;reshape | solution.py:135
  564.2 0.9 fusion.34
  565.1 0.8 copy-done.3
  566.0 7.9 %fusion.22 = f32[2,256,40,64]{1,3,2,0:T(8,128)} fusion(bf16[2,256,40,64]{1,3,2,0:T(8,128)(2,1)S(1)} %copy-done.3, f32[2,40,64,256]{3,2,1,0:T(8,128)S(1)} %fusion.34, f32[2,256,40]{1,2,0:T(8,128)S(1)} %copy-done.9, f32[40]{0:T(128)S(1)} %copy-done.25, f32[2,40,256]{2,1,0:T(8,128)S(1)} %copy.112, f32[2,40,256]{2,1,0:T(8,128)S(1)} %copy_bitcast_fusion, ...), kind=kOutput, calls=%fused_computation.37 | convolution fusion | flops 703856640 | bytes 13942944 | tf_op jit(solution)/shard_map/chkr,crhp->ckhp/dot_general | solution.py:54
  573.9 8.6 %copy.125 = f32[2,256,40,64]{3,2,1,0:T(8,128)} copy(f32[2,256,40,64]{1,3,2,0:T(8,128)} %fusion.22) | data formatting | bytes 10485760 | tf_op jit(solution)/shard_map/stack;reshape | solution.py:135
  582.5 9.6 %reshape.261 = f32[1,512,2560]{2,1,0:T(8,128)} reshape(f32[2,256,40,64]{3,2,1,0:T(8,128)} %copy.125) | data formatting | bytes 10485760 | tf_op jit(solution)/shard_map/stack;reshape | solution.py:135
  592.1 11.9 %multiply_reduce_fusion = (f32[2,512]{1,0:T(2,128)S(1)}, f32[2,512,2560]{2,1,0:T(8,128)}) fusion(bf16[2,512,2560]{2,1,0:T(8,128)(2,1)} %param.16, f32[1,512,2560]{2,1,0:T(8,128)} %reshape.261, f32[1,512,2560]{2,1,0:T(8,128)} %reshape.260), kind=kLoop, calls=%fused_computation.16 | loop fusion | flops 23591936 | bytes 26218496 | tf_op jit(solution)/shard_map/reduce_sum | solution.py:137
  604.0 2.4 psum.14
  606.4 7.3 %multiply_convert_fusion.4 = bf16[2,512,2560]{2,1,0:T(8,128)(2,1)} fusion(f32[2,512,2560]{2,1,0:T(8,128)} %get-tuple-element.134, f32[2560]{0:T(1024)S(1)} %copy-done.15, f32[2,512]{1,0:T(2,128)S(1)} %add_rsqrt_fusion), kind=kLoop, calls=%fused_computation.15 | loop fusion | flops 7864320 | bytes 15742976 | tf_op jit(solution)/shard_map/convert_element_type | solution.py:139
  613.7 2.2 gather_fusion.1
  616.0 2.3 all_gather.19
  618.6 1.1 reshape.226
  619.7 3.8 all-to-all-start
  623.6 17.6 %all-to-all-done = bf16[16,4,5120]{2,1,0:T(4,128)(2,1)S(1)} async-done(((bf16[16,4,5120]{2,1,0:T(4,128)(2,1)}), bf16[16,4,5120]{2,1,0:T(4,128)(2,1)S(1)}, u32[]{:S(2)}, u32[]{:S(2)}) %all-to-all-start) | async-done | bytes 655392 | tf_op jit(solution)/shard_map/all_to_all | solution.py:159
  641.2 3.6 fusion.61
  644.8 2.5 psum.15
  647.9 4.4 all-to-all-start.1
  652.5 7.2 %all-to-all-done.1 = f32[16,1,4]{2,1,0:T(1,128)S(1)} async-done(((f32[16,1,4]{2,1,0:T(1,128)}), f32[16,1,4]{2,1,0:T(1,128)S(1)}, u32[]{:S(2)}, u32[]{:S(2)}) %all-to-all-start.1) | async-done | bytes 288 | tf_op jit(solution)/shard_map/all_to_all | solution.py:76
  660.9 0.8 gather_fusion
  (125 shorter events, 24.6 us)
Async XLA Ops:
  7.2 634.1 %copy-start = (bf16[1,512]{1,0:T(2,128)(2,1)S(1)}, bf16[1,512]{1,0:T(2,128)(2,1)}, u32[]{:S(2)}) copy-start(bf16[1,512]{1,0:T(2,128)(2,1)} %param.27) | copy-start | bytes 3076
  7.2 478.9 %all-gather.5.cloned.1.call-start = ((), (), s32[]{:S(2)}) async-start(), calls=%async_computation.2 | async-start | bytes 44564480 | tf_op jit(solution)/shard_map/all_gather | solution.py:15
  14.6 20.3 %copy-start.13 = (f32[2,40]{1,0:T(2,128)}, f32[2,40]{1,0:T(2,128)S(1)}, u32[]{:S(2)}) copy-start(f32[2,40]{1,0:T(2,128)S(1)} %get-tuple-element.122) | copy-start | bytes 964
  44.8 4.4 copy-start.2
  44.8 4.4 copy-start.19
  44.8 4.4 copy-start.20
  44.8 4.4 copy-start.21
  44.8 4.4 copy-start.22
  51.2 2.5 copy-start.14
  102.9 3.9 copy-start.26
  534.6 1.6 copy-start.6
  534.6 1.6 copy-start.16
  535.9 1.8 copy-start.4
  535.9 1.9 copy-start.8
  535.9 1.9 copy-start.10
  535.9 1.9 copy-start.11
  535.9 1.9 copy-start.25
  554.4 9.8 %copy-start.1 = (f32[40,64,128]{2,1,0:T(8,128)S(1)}, f32[40,64,128]{2,1,0:T(8,128)}, u32[]{:S(2)}) copy-start(f32[40,64,128]{2,1,0:T(8,128)} %get-tuple-element.142) | copy-start | bytes 3932164
  554.4 9.8 %copy-start.5 = (f32[1,40,64,128]{3,2,1,0:T(8,128)S(1)}, f32[1,40,64,128]{3,2,1,0:T(8,128)}, u32[]{:S(2)}) copy-start(f32[1,40,64,128]{3,2,1,0:T(8,128)} %get-tuple-element.138) | copy-start | bytes 3932164
  564.1 1.7 copy-start.3
  564.1 1.8 copy-start.7
  564.1 1.8 copy-start.9
  564.1 1.8 copy-start.12
  592.1 14.4 %copy-start.15 = (f32[2560]{0:T(1024)S(1)}, f32[2560]{0:T(1024)}, u32[]{:S(2)}) copy-start(f32[2560]{0:T(1024)} %param.22) | copy-start | bytes 30724
  606.4 9.5 %copy-start.24 = (pred[64]{0:T(512)(128)(4,1)S(1)}, pred[64]{0:T(512)(128)(4,1)}, u32[]{:S(2)}) copy-start(pred[64]{0:T(512)(128)(4,1)} %broadcast_in_dim.35) | copy-start | bytes 196
  606.4 11.9 %copy-start.23 = (s32[64]{0:T(128)S(1)}, s32[64]{0:T(128)}, u32[]{:S(2)}) copy-start(s32[64]{0:T(128)} %multiply_add_fusion) | copy-start | bytes 772
  613.7 9.8 %copy-start.17 = (s32[2,32]{1,0:T(2,128)S(1)}, s32[2,32]{1,0:T(2,128)}, u32[]{:S(2)}) copy-start(s32[2,32]{1,0:T(2,128)} %param.24) | copy-start | bytes 772
  613.7 9.9 %copy-start.27 = (s32[64]{0:T(128)S(1)}, s32[64]{0:T(128)}, u32[]{:S(2)}) copy-start(s32[64]{0:T(128)} %copy-done.26) | copy-start | bytes 772
  613.7 27.5 %copy-start.18 = (f32[1,512]{1,0:T(1,128)S(1)}, f32[1,512]{1,0:T(1,128)}, u32[]{:S(2)}) copy-start(f32[1,512]{1,0:T(1,128)} %param.26) | copy-start | bytes 6148
  619.7 21.5 %all-to-all-start = ((bf16[16,4,5120]{2,1,0:T(4,128)(2,1)}), bf16[16,4,5120]{2,1,0:T(4,128)(2,1)S(1)}, u32[]{:S(2)}, u32[]{:S(2)}) async-start(bf16[16,4,5120]{2,1,0:T(4,128)(2,1)} %reshape.226), calls=%async_computation | async-start | bytes 1310720 | tf_op jit(solution)/shard_map/all_to_all | solution.py:159
  647.9 11.7 %all-to-all-start.1 = ((f32[16,1,4]{2,1,0:T(1,128)}), f32[16,1,4]{2,1,0:T(1,128)S(1)}, u32[]{:S(2)}, u32[]{:S(2)}) async-start(f32[16,1,4]{2,1,0:T(1,128)} %copy.118), calls=%async_computation.1 | async-start | bytes 16384 | tf_op jit(solution)/shard_map/all_to_all | solution.py:76
Sparse Core Ops, SparseCore 0:
  53.2 432.8 all-gather.4
where the time goes:
time: 672 us; the launch traced here: 669 us
  waiting for transfers between devices  400 us (60%)
  local copies, waits for them, and re-layouts  89 us (13%)
  other arithmetic  76.8 us (11%)
  blocking collectives  52.1 us (8%)
  matrix products  27.9 us (4%)
  between operations  14.5 us (2%)
  starting transfers between devices  8.28 us (1%)
    all_gather x1, waiting for transfers between devices, carried_in(): everything = jax.tree.map(lambda part: lax.all_gather(part, axis), value)  375 us
    all_gather x1, blocking collectives, carried_in(): everything = jax.tree.map(lambda part: lax.all_gather(part, axis), value)  44.9 us
    select_n x16, other arithmetic, hop(): return jax.tree.map(lambda a, b: jnp.where(reached, a, b), new, before)  37.7 us
    another operation x4, local copies, waits for them, and re-layouts, body(): y_full = jnp.stack(outputs)  36.6 us
    another operation x4, local copies, waits for them, and re-layouts, block_parts(): x_blocks = x_seq.reshape(block_count, BLOCK, head_count, -1)  23.5 us
    all_to_all x1, waiting for transfers between devices, body(): lax.all_to_all(routed_full, 'seq', split_axis=0, concat_axis=0, tiled=True)  17.6 us
    dot_general x2, matrix products, diagonal_part(): jnp.einsum('chkr,crhp->ckhp', weights, x_blocks, preferred_element_type=j...  15.8 us
  transfers between devices with their start and end apart: 3, of which 3 were waited for; matrix products, arithmetic and copies ran while one was open for 2% of the time, Pallas kernels for 0%

commit v1 on v0

--- a/solution.py
+++ b/solution.py
@@ -8,6 +8,22 @@
 BLOCK = 256
 CAP = 4
 norm_eps = 1e-05
+
+
+def exchange_in_pairs(shard, axis, split, join):
+    ways, here = (lax.axis_size(axis), lax.axis_index(axis))
+    width = shard.shape[split] // ways
+    shape = list(shard.shape)
+    shape[split] = width
+    height = shape[join]
+    shape[join] = height * ways
+    full = jnp.zeros(shape, shard.dtype)
+    for mask in range(ways):
+        part = lax.dynamic_slice_in_dim(shard, (here ^ mask) * width, width, axis=split)
+        if mask:
+            part = lax.ppermute(part, axis, [(d, d ^ mask) for d in range(ways)])
+        full = lax.dynamic_update_slice_in_dim(full, part, (here ^ mask) * height, axis=join)
+    return full
 
 
 def carried_in(value, axis, combine, identity):
@@ -155,12 +171,7 @@
         .reshape(experts, CAP, -1)
     )
     returned = finish_values(
-        value_terms(
-            lax.all_to_all(routed_full, "seq", split_axis=0, concat_axis=0, tiled=True),
-            value_w1,
-            value_b1,
-            value_w2,
-        )
+        value_terms(exchange_in_pairs(routed_full, "seq", 0, 0), value_w1, value_b1, value_w2)
     )
     picked = jnp.take(returned.reshape(-1), slot_index)
     values = picked.reshape(seq_count, goal_dev)

time: 672 us -> 697 us (1.037)
  starting transfers between devices: 8.28 us -> 29.2 us
  local copies, waits for them, and re-layouts: 89 us -> 103 us
  waiting for transfers between devices: 400 us -> 390 us
    ppermute x0 -> x15, starting transfers between devices: none -> 24.5 us  [exchange_in_pairs(): part = lax.ppermute(part, axis, [(d, d ^ mask) for d in range(ways)])]
    all_to_all x1 -> x0, waiting for transfers between devices: 17.6 us -> none  [body(): lax.all_to_all(routed_full, 'seq', split_axis=0, concat_axis=0, tiled=True)]
    dynamic_update_slice x0 -> x16, local copies, waits for them, and re-layouts: none -> 13.5 us  [exchange_in_pairs(): lax.dynamic_update_slice_in_dim(full, part, (here ^ mask) * height, axis=...]
    ppermute x0 -> x15, waiting for transfers between devices: none -> 7.06 us  [exchange_in_pairs(): part = lax.ppermute(part, axis, [(d, d ^ mask) for d in range(ways)])]
  transfers between devices with their start and end apart: 3 -> 17, of which waited for: 3 -> 6; matrix products, arithmetic and copies ran while one was open for 2% -> 4% of each run, Pallas kernels for 0% -> 0%
where the time goes in v1:
time: 697 us; the launch traced here: 694 us
  waiting for transfers between devices  390 us (56%)
  local copies, waits for them, and re-layouts  103 us (15%)
  other arithmetic  76.8 us (11%)
  blocking collectives  52.3 us (8%)
  starting transfers between devices  29.2 us (4%)
  matrix products  28 us (4%)
  between operations  14.8 us (2%)
    all_gather x1, waiting for transfers between devices, carried_in(): everything = jax.tree.map(lambda part: lax.all_gather(part, axis), value)  375 us
    all_gather x1, blocking collectives, carried_in(): everything = jax.tree.map(lambda part: lax.all_gather(part, axis), value)  44.9 us
    select_n x16, other arithmetic, hop(): return jax.tree.map(lambda a, b: jnp.where(reached, a, b), new, before)  37.7 us
    another operation x4, local copies, waits for them, and re-layouts, body(): y_full = jnp.stack(outputs)  36.6 us
    ppermute x15, starting transfers between devices, exchange_in_pairs(): part = lax.ppermute(part, axis, [(d, d ^ mask) for d in range(ways)])  24.5 us
    another operation x4, local copies, waits for them, and re-layouts, block_parts(): x_blocks = x_seq.reshape(block_count, BLOCK, head_count, -1)  23.5 us
    dot_general x2, matrix products, diagonal_part(): jnp.einsum('chkr,crhp->ckhp', weights, x_blocks, preferred_element_type=j...  15.8 us
  transfers between devices with their start and end apart: 17, of which 6 were waited for; matrix products, arithmetic and copies ran while one was open for 4% of the time, Pallas kernels for 0%

profile of v1, /device:TPU:0, one launch (start us, length us, event | category | flops | bytes accessed | tf_op | source)
XLA Modules:
  0.0 694.2 jit_solution(11729738638569959172)
XLA Ops:
  9.2 1.2 reduce-window.14
  12.4 1.2 reduce-window.16
  15.7 4.4 fusion.87
  20.0 7.5 %reshape.263 = bf16[2,256,40,64]{3,2,1,0:T(8,128)(2,1)} reshape(bf16[1,512,2560]{2,1,0:T(8,128)(2,1)} %get-tuple-element.139) | data formatting | bytes 5242880 | tf_op jit(solution)/shard_map/reshape;squeeze | solution.py:50
  27.6 6.4 copy.159
  34.0 1.0 fusion.89
  35.2 4.4 reshape.264
  39.6 5.2 copy.167
  44.8 3.5 fusion.29
  49.3 1.9 slice_add_fusion
  51.2 1.8 pad_maximum_fusion
  57.8 44.9 %all-gather.2 = f32[16,2,40]{2,1,0:T(2,128)} all-gather(f32[1,2,40]{2,1,0:T(2,128)S(1)} %maximum_bitcast_fusion), channel_id=2, replica_groups=mesh['seq'=16,'head'=2] {'seq'}, dimensions={0}, use_global_device_ids=true | all-gather | bytes 5440 | tf_op jit(solution)/shard_map/all_gather | solution.py:31
  104.1 1.3 subtract_exponential_fusion.1
  107.6 1.0 fusion.88
  108.5 1.0 fusion.91
  109.6 1.0 fusion.92
  110.6 375.5 %all-gather.5.cloned.1.call-done = f32[32,40,64,128]{3,2,1,0:T(8,128)} async-done(((f32[2,40,64,128]{3,2,1,0:T(8,128)}), f32[32,40,64,128]{3,2,1,0:T(8,128)}) %all-gather.5.cloned.1.call-update) | async-done | bytes 41943056 | tf_op jit(solution)/shard_map/all_gather | solution.py:31
  486.1 48.5 %while.14 = (s32[]{:T(128)}, f32[2,40,64,128]{3,2,1,0:T(8,128)S(1)}, s32[]{:T(128)}, f32[16,2,40]{2,1,0:T(2,128)}, f32[16,2,40,64,128]{4,3,2,1,0:T(8,128)}, /*index=5*/s32[]{:T(128)}, s32[]{:T(128)}) while((s32[]{:T(128)}, f32[2,40,64,128]{3,2,1,0:T(8,128)S(1)}, s32[]{:T(128)}, f32[16,2,40]{2,1,0:T(2,128)}, ...), condition=%wide.region_8.9_spmd.clone, body=%wide.region_7.8_spmd.clone.sunk | while | flops 2621444 | bytes 7865385 | solution.py:43
  486.7 2.4 fusion.106
  489.8 2.4 fusion.106
  492.8 2.4 fusion.106
  495.8 2.4 fusion.106
  498.9 2.4 fusion.106
  501.9 2.4 fusion.106
  505.0 2.4 fusion.106
  508.0 2.4 fusion.106
  511.0 2.4 fusion.106
  514.0 2.4 fusion.106
  517.1 2.4 fusion.106
  520.1 2.4 fusion.106
  523.1 2.4 fusion.106
  526.1 2.4 fusion.106
  529.2 2.4 fusion.106
  532.2 2.4 fusion.106
  534.6 1.3 slice_bitcast_fusion.1
  537.8 7.9 %fusion.20 = f32[2,256,40,64]{1,3,2,0:T(8,128)} fusion(bf16[2,256,40,64]{1,3,2,0:T(8,128)(2,1)S(1)} %copy-done.4, f32[2,40,64,256]{3,2,1,0:T(8,128)S(1)} %fusion.33, f32[40]{0:T(128)S(1)} %copy-done.25, f32[2,256,40]{1,2,0:T(8,128)S(1)} %copy-done.10, f32[2,40,256]{2,1,0:T(8,128)S(1)} %copy.157, f32[2,40,256]{2,1,0:T(8,128)S(1)} %copy_bitcast_fusion.1, ...), kind=kOutput, calls=%fused_computation.35 | convolution fusion | flops 703856640 | bytes 13942944 | tf_op jit(solution)/shard_map/chkr,crhp->ckhp/dot_general | solution.py:70
  545.7 8.6 %copy.199 = f32[2,256,40,64]{3,2,1,0:T(8,128)} copy(f32[2,256,40,64]{1,3,2,0:T(8,128)} %fusion.20) | data formatting | bytes 10485760 | tf_op jit(solution)/shard_map/stack;reshape | solution.py:151
  554.4 9.7 %reshape.260 = f32[1,512,2560]{2,1,0:T(8,128)} reshape(f32[2,256,40,64]{3,2,1,0:T(8,128)} %copy.199) | data formatting | bytes 10485760 | tf_op jit(solution)/shard_map/stack;reshape | solution.py:151
  566.0 7.9 %fusion.22 = f32[2,256,40,64]{1,3,2,0:T(8,128)} fusion(bf16[2,256,40,64]{1,3,2,0:T(8,128)(2,1)S(1)} %copy-done.3, f32[2,40,64,256]{3,2,1,0:T(8,128)S(1)} %fusion.34, f32[2,256,40]{1,2,0:T(8,128)S(1)} %copy-done.9, f32[40]{0:T(128)S(1)} %copy-done.25, f32[2,40,256]{2,1,0:T(8,128)S(1)} %copy.172, f32[2,40,256]{2,1,0:T(8,128)S(1)} %copy_bitcast_fusion, ...), kind=kOutput, calls=%fused_computation.37 | convolution fusion | flops 703856640 | bytes 13942944 | tf_op jit(solution)/shard_map/chkr,crhp->ckhp/dot_general | solution.py:70
  573.9 8.6 %copy.200 = f32[2,256,40,64]{3,2,1,0:T(8,128)} copy(f32[2,256,40,64]{1,3,2,0:T(8,128)} %fusion.22) | data formatting | bytes 10485760 | tf_op jit(solution)/shard_map/stack;reshape | solution.py:151
  582.5 9.6 %reshape.261 = f32[1,512,2560]{2,1,0:T(8,128)} reshape(f32[2,256,40,64]{3,2,1,0:T(8,128)} %copy.200) | data formatting | bytes 10485760 | tf_op jit(solution)/shard_map/stack;reshape | solution.py:151
  592.1 11.9 %multiply_reduce_fusion = (f32[2,512]{1,0:T(2,128)S(1)}, f32[2,512,2560]{2,1,0:T(8,128)}) fusion(bf16[2,512,2560]{2,1,0:T(8,128)(2,1)} %param.16, f32[1,512,2560]{2,1,0:T(8,128)} %reshape.261, f32[1,512,2560]{2,1,0:T(8,128)} %reshape.260), kind=kLoop, calls=%fused_computation.16 | loop fusion | flops 23591936 | bytes 26218496 | tf_op jit(solution)/shard_map/reduce_sum | solution.py:153
  604.0 2.4 psum.14
  606.4 7.3 %multiply_convert_fusion.4 = bf16[2,512,2560]{2,1,0:T(8,128)(2,1)} fusion(f32[2,512,2560]{2,1,0:T(8,128)} %get-tuple-element.134, f32[2560]{0:T(1024)S(1)} %copy-done.15, f32[2,512]{1,0:T(2,128)S(1)} %add_rsqrt_fusion), kind=kLoop, calls=%fused_computation.15 | loop fusion | flops 7864320 | bytes 15742976 | tf_op jit(solution)/shard_map/convert_element_type | solution.py:155
  613.7 2.2 gather_fusion.1
  616.0 2.5 all_gather.19
  619.5 1.5 collective-permute-start
  621.8 1.5 collective-permute-start.2
  623.5 3.0 collective-permute-start.4
  627.3 2.5 collective-permute-start.6
  629.9 1.5 collective-permute-start.7
  631.4 2.3 collective-permute-start.8
  633.7 1.5 collective-permute-start.9
  635.7 2.4 collective-permute-start.10
  638.0 1.4 collective-permute-start.11
  639.4 5.2 collective-permute-done.7
  644.7 2.2 collective-permute-start.12
  646.9 1.1 collective-permute-done.8
  648.0 1.5 collective-permute-start.13
  649.8 2.4 collective-permute-start.14
  665.9 3.7 fusion.55
  669.6 2.5 psum.15
  672.8 4.6 all-to-all-start
  677.5 7.2 %all-to-all-done = f32[16,1,4]{2,1,0:T(1,128)S(1)} async-done(((f32[16,1,4]{2,1,0:T(1,128)}), f32[16,1,4]{2,1,0:T(1,128)S(1)}, u32[]{:S(2)}, u32[]{:S(2)}) %all-to-all-start) | async-done | bytes 288 | tf_op jit(solution)/shard_map/all_to_all | solution.py:92
  (187 shorter events, 50.2 us)
Async XLA Ops:
  7.2 658.8 %copy-start = (bf16[1,512]{1,0:T(2,128)(2,1)S(1)}, bf16[1,512]{1,0:T(2,128)(2,1)}, u32[]{:S(2)}) copy-start(bf16[1,512]{1,0:T(2,128)(2,1)} %param.27) | copy-start | bytes 3076
  7.2 478.9 %all-gather.5.cloned.1.call-start = ((), (), s32[]{:S(2)}) async-start(), calls=%async_computation.1 | async-start | bytes 44564480 | tf_op jit(solution)/shard_map/all_gather | solution.py:31
  14.6 20.3 %copy-start.13 = (f32[2,40]{1,0:T(2,128)}, f32[2,40]{1,0:T(2,128)S(1)}, u32[]{:S(2)}) copy-start(f32[2,40]{1,0:T(2,128)S(1)} %get-tuple-element.122) | copy-start | bytes 964
  44.8 4.4 copy-start.2
  44.8 4.4 copy-start.19
  44.8 4.4 copy-start.20
  44.8 4.4 copy-start.21
  44.8 4.4 copy-start.22
  51.2 2.5 copy-start.14
  102.9 3.9 copy-start.26
  534.6 1.6 copy-start.6
  534.6 1.6 copy-start.16
  535.9 1.8 copy-start.4
  535.9 1.9 copy-start.8
  535.9 1.9 copy-start.10
  535.9 1.9 copy-start.11
  535.9 1.9 copy-start.25
  554.4 9.8 %copy-start.1 = (f32[40,64,128]{2,1,0:T(8,128)S(1)}, f32[40,64,128]{2,1,0:T(8,128)}, u32[]{:S(2)}) copy-start(f32[40,64,128]{2,1,0:T(8,128)} %get-tuple-element.142) | copy-start | bytes 3932164
  554.4 9.8 %copy-start.5 = (f32[1,40,64,128]{3,2,1,0:T(8,128)S(1)}, f32[1,40,64,128]{3,2,1,0:T(8,128)}, u32[]{:S(2)}) copy-start(f32[1,40,64,128]{3,2,1,0:T(8,128)} %get-tuple-element.138) | copy-start | bytes 3932164
  564.1 1.7 copy-start.3
  564.1 1.8 copy-start.7
  564.1 1.8 copy-start.9
  564.1 1.8 copy-start.12
  592.1 14.4 %copy-start.15 = (f32[2560]{0:T(1024)S(1)}, f32[2560]{0:T(1024)}, u32[]{:S(2)}) copy-start(f32[2560]{0:T(1024)} %param.22) | copy-start | bytes 30724
  606.4 9.5 %copy-start.24 = (pred[64]{0:T(512)(128)(4,1)S(1)}, pred[64]{0:T(512)(128)(4,1)}, u32[]{:S(2)}) copy-start(pred[64]{0:T(512)(128)(4,1)} %broadcast_in_dim.38) | copy-start | bytes 196
  606.4 12.1 %copy-start.23 = (s32[64]{0:T(128)S(1)}, s32[64]{0:T(128)}, u32[]{:S(2)}) copy-start(s32[64]{0:T(128)} %multiply_add_fusion) | copy-start | bytes 772
  613.7 21.5 %copy-start.17 = (s32[2,32]{1,0:T(2,128)S(1)}, s32[2,32]{1,0:T(2,128)}, u32[]{:S(2)}) copy-start(s32[2,32]{1,0:T(2,128)} %param.24) | copy-start | bytes 772
  613.7 38.4 %copy-start.27 = (s32[64]{0:T(128)S(1)}, s32[64]{0:T(128)}, u32[]{:S(2)}) copy-start(s32[64]{0:T(128)} %copy-done.26) | copy-start | bytes 772
  616.0 49.9 %copy-start.18 = (f32[1,512]{1,0:T(1,128)S(1)}, f32[1,512]{1,0:T(1,128)}, u32[]{:S(2)}) copy-start(f32[1,512]{1,0:T(1,128)} %param.26) | copy-start | bytes 6148
  619.5 7.4 %collective-permute-start = (bf16[1,4,5120]{2,0,1:T(2,128)(2,1)S(1)}, bf16[1,4,5120]{2,0,1:T(2,128)(2,1)S(1)}, u32[]{:S(2)}, u32[]{:S(2)}) collective-permute-start(bf16[1,4,5120]{2,0,1:T(2,128)(2,1)S(1)} %copy.208), channel_id=1, source_target_pairs={{0,2},{2,0},{4,6},{6,4},{8,10},{10,8},{12,14},{14,12},{16,18},{18,... | collective-permute-start | bytes 122888 | tf_op jit(solution)/shard_map/ppermute | solution.py:24
  621.1 6.3 collective-permute-start.1
  621.8 8.1 %collective-permute-start.2 = (bf16[1,4,5120]{2,0,1:T(2,128)(2,1)S(1)}, bf16[1,4,5120]{2,0,1:T(2,128)(2,1)S(1)}, u32[]{:S(2)}, u32[]{:S(2)}) collective-permute-start(bf16[1,4,5120]{2,0,1:T(2,128)(2,1)S(1)} %copy.210), channel_id=1, source_target_pairs={{0,6},{2,4},{4,2},{6,0},{8,14},{10,12},{12,10},{14,8},{16,22},{18,... | collective-permute-start | bytes 122888 | tf_op jit(solution)/shard_map/ppermute | solution.py:24
  623.4 8.0 %collective-permute-start.3 = (bf16[1,4,5120]{2,0,1:T(2,128)(2,1)S(1)}, bf16[1,4,5120]{2,0,1:T(2,128)(2,1)S(1)}, u32[]{:S(2)}, u32[]{:S(2)}) collective-permute-start(bf16[1,4,5120]{2,0,1:T(2,128)(2,1)S(1)} %copy.211), channel_id=1, source_target_pairs={{0,8},{2,10},{4,12},{6,14},{8,0},{10,2},{12,4},{14,6},{16,24},{18,... | collective-permute-start | bytes 122888 | tf_op jit(solution)/shard_map/ppermute | solution.py:24
  623.5 10.2 %collective-permute-start.4 = (bf16[1,4,5120]{2,0,1:T(2,128)(2,1)S(1)}, bf16[1,4,5120]{2,0,1:T(2,128)(2,1)S(1)}, u32[]{:S(2)}, u32[]{:S(2)}) collective-permute-start(bf16[1,4,5120]{2,0,1:T(2,128)(2,1)S(1)} %copy.212), channel_id=1, source_target_pairs={{0,10},{2,8},{4,14},{6,12},{8,2},{10,0},{12,6},{14,4},{16,26},{18,... | collective-permute-start | bytes 122888 | tf_op jit(solution)/shard_map/ppermute | solution.py:24
  626.8 8.8 %collective-permute-start.5 = (bf16[1,4,5120]{2,0,1:T(2,128)(2,1)S(1)}, bf16[1,4,5120]{2,0,1:T(2,128)(2,1)S(1)}, u32[]{:S(2)}, u32[]{:S(2)}) collective-permute-start(bf16[1,4,5120]{2,0,1:T(2,128)(2,1)S(1)} %copy.213), channel_id=1, source_target_pairs={{0,12},{2,14},{4,8},{6,10},{8,4},{10,6},{12,0},{14,2},{16,28},{18,... | collective-permute-start | bytes 122888 | tf_op jit(solution)/shard_map/ppermute | solution.py:24
  627.3 10.7 %collective-permute-start.6 = (bf16[1,4,5120]{2,0,1:T(2,128)(2,1)S(1)}, bf16[1,4,5120]{2,0,1:T(2,128)(2,1)S(1)}, u32[]{:S(2)}, u32[]{:S(2)}) collective-permute-start(bf16[1,4,5120]{2,0,1:T(2,128)(2,1)S(1)} %copy.214), channel_id=1, source_target_pairs={{0,14},{2,12},{4,10},{6,8},{8,6},{10,4},{12,2},{14,0},{16,30},{18,... | collective-permute-start | bytes 122888 | tf_op jit(solution)/shard_map/ppermute | solution.py:24
  629.9 14.8 %collective-permute-start.7 = (bf16[1,4,5120]{2,0,1:T(2,128)(2,1)S(1)}, bf16[1,4,5120]{2,0,1:T(2,128)(2,1)S(1)}, u32[]{:S(2)}, u32[]{:S(2)}) collective-permute-start(bf16[1,4,5120]{2,0,1:T(2,128)(2,1)S(1)} %copy.215), channel_id=1, source_target_pairs={{0,16},{2,18},{4,20},{6,22},{8,24},{10,26},{12,28},{14,30},{16,0},... | collective-permute-start | bytes 122888 | tf_op jit(solution)/shard_map/ppermute | solution.py:24
  631.4 16.6 %collective-permute-start.8 = (bf16[1,4,5120]{2,0,1:T(2,128)(2,1)S(1)}, bf16[1,4,5120]{2,0,1:T(2,128)(2,1)S(1)}, u32[]{:S(2)}, u32[]{:S(2)}) collective-permute-start(bf16[1,4,5120]{2,0,1:T(2,128)(2,1)S(1)} %copy.216), channel_id=1, source_target_pairs={{0,18},{2,16},{4,22},{6,20},{8,26},{10,24},{12,30},{14,28},{16,2},... | collective-permute-start | bytes 122888 | tf_op jit(solution)/shard_map/ppermute | solution.py:24
  633.7 16.1 %collective-permute-start.9 = (bf16[1,4,5120]{2,0,1:T(2,128)(2,1)S(1)}, bf16[1,4,5120]{2,0,1:T(2,128)(2,1)S(1)}, u32[]{:S(2)}, u32[]{:S(2)}) collective-permute-start(bf16[1,4,5120]{2,0,1:T(2,128)(2,1)S(1)} %copy.217), channel_id=1, source_target_pairs={{0,20},{2,22},{4,16},{6,18},{8,28},{10,30},{12,24},{14,26},{16,4},... | collective-permute-start | bytes 122888 | tf_op jit(solution)/shard_map/ppermute | solution.py:24
  635.7 26.0 %collective-permute-start.10 = (bf16[1,4,5120]{2,0,1:T(2,128)(2,1)S(1)}, bf16[1,4,5120]{2,0,1:T(2,128)(2,1)S(1)}, u32[]{:S(2)}, u32[]{:S(2)}) collective-permute-start(bf16[1,4,5120]{2,0,1:T(2,128)(2,1)S(1)} %copy.218), channel_id=1, source_target_pairs={{0,22},{2,20},{4,18},{6,16},{8,30},{10,28},{12,26},{14,24},{16,6},... | collective-permute-start | bytes 122888 | tf_op jit(solution)/shard_map/ppermute | solution.py:24
  638.0 24.4 %collective-permute-start.11 = (bf16[1,4,5120]{2,0,1:T(2,128)(2,1)S(1)}, bf16[1,4,5120]{2,0,1:T(2,128)(2,1)S(1)}, u32[]{:S(2)}, u32[]{:S(2)}) collective-permute-start(bf16[1,4,5120]{2,0,1:T(2,128)(2,1)S(1)} %copy.219), channel_id=1, source_target_pairs={{0,24},{2,26},{4,28},{6,30},{8,16},{10,18},{12,20},{14,22},{16,8},... | collective-permute-start | bytes 122888 | tf_op jit(solution)/shard_map/ppermute | solution.py:24
  644.7 18.6 %collective-permute-start.12 = (bf16[1,4,5120]{2,0,1:T(2,128)(2,1)S(1)}, bf16[1,4,5120]{2,0,1:T(2,128)(2,1)S(1)}, u32[]{:S(2)}, u32[]{:S(2)}) collective-permute-start(bf16[1,4,5120]{2,0,1:T(2,128)(2,1)S(1)} %copy.220), channel_id=1, source_target_pairs={{0,26},{2,24},{4,30},{6,28},{8,18},{10,16},{12,22},{14,20},{16,10}... | collective-permute-start | bytes 122888 | tf_op jit(solution)/shard_map/ppermute | solution.py:24
  648.0 16.2 %collective-permute-start.13 = (bf16[1,4,5120]{2,0,1:T(2,128)(2,1)S(1)}, bf16[1,4,5120]{2,0,1:T(2,128)(2,1)S(1)}, u32[]{:S(2)}, u32[]{:S(2)}) collective-permute-start(bf16[1,4,5120]{2,0,1:T(2,128)(2,1)S(1)} %copy.221), channel_id=1, source_target_pairs={{0,28},{2,30},{4,24},{6,26},{8,20},{10,22},{12,16},{14,18},{16,12}... | collective-permute-start | bytes 122888 | tf_op jit(solution)/shard_map/ppermute | solution.py:24
  649.8 15.3 %collective-permute-start.14 = (bf16[1,4,5120]{2,0,1:T(2,128)(2,1)S(1)}, bf16[1,4,5120]{2,0,1:T(2,128)(2,1)S(1)}, u32[]{:S(2)}, u32[]{:S(2)}) collective-permute-start(bf16[1,4,5120]{2,0,1:T(2,128)(2,1)S(1)} %copy.222), channel_id=1, source_target_pairs={{0,30},{2,28},{4,26},{6,24},{8,22},{10,20},{12,18},{14,16},{16,14}... | collective-permute-start | bytes 122888 | tf_op jit(solution)/shard_map/ppermute | solution.py:24
  672.8 11.9 %all-to-all-start = ((f32[16,1,4]{2,1,0:T(1,128)}), f32[16,1,4]{2,1,0:T(1,128)S(1)}, u32[]{:S(2)}, u32[]{:S(2)}) async-start(f32[16,1,4]{2,1,0:T(1,128)} %copy.193), calls=%async_computation | async-start | bytes 16384 | tf_op jit(solution)/shard_map/all_to_all | solution.py:92
Sparse Core Ops, SparseCore 0:
  53.2 432.8 all-gather.4
